TPU v7x, 32 devices: a whole 2x2x4 slice. The times are simulated.
32 devices in a mesh: dp: 2 (over x), ctx: 4 (over y, core), tensor: 4 (over z).
Axes of the slice: x: 2, y: 2, z: 4, core: 2. Of those that a mesh axis runs over, the one named last changes fastest.
Arguments:
- hidden_in: bfloat16 [2, 2048, 768], P('dp', 'ctx'), may hold values from -6 to 6
- encoder_out: bfloat16 [2, 2048, 768], P('dp', 'ctx'), may hold values from -6 to 6
- dec_segments: int32 [2, 2048], P('dp'), may hold values from 0 to 7, as said below
- enc_segments: int32 [2, 2048], P('dp'), may hold values from 0 to 7, as said below
- gain_self: bfloat16 [768], replicated, may hold values from 0.5 to 1.5
- gain_cross: bfloat16 [768], replicated, may hold values from 0.5 to 1.5
- gain_feed: bfloat16 [768], replicated, may hold values from 0.5 to 1.5
- self_query: bfloat16 [768, 768], P(None, 'tensor'), may hold values from -0.02734375 to 0.02734375
- self_key: bfloat16 [768, 768], P(None, 'tensor'), may hold values from -0.21875 to 0.21875
- self_value: bfloat16 [768, 768], P(None, 'tensor'), may hold values from -0.21875 to 0.21875
- self_output: bfloat16 [768, 768], P('tensor'), may hold values from -0.75 to 0.75
- bias_table: bfloat16 [32, 12], P(None, 'tensor'), may hold values from -4 to 4
- cross_query: bfloat16 [768, 768], P(None, 'tensor'), may hold values from -0.02734375 to 0.02734375
- cross_key: bfloat16 [768, 768], P(None, 'tensor'), may hold values from -0.21875 to 0.21875
- cross_value: bfloat16 [768, 768], P(None, 'tensor'), may hold values from -0.21875 to 0.21875
- cross_output: bfloat16 [768, 768], P('tensor'), may hold values from -0.75 to 0.75
- hidden_up: bfloat16 [768, 3072], P(None, 'tensor'), may hold values from -0.21875 to 0.21875
- hidden_down: bfloat16 [3072, 768], P('tensor'), may hold values from -0.109375 to 0.109375
- out_grad: bfloat16 [2, 2048, 768], P('dp', 'ctx'), may hold values from -6 to 6
Outputs:
- layer_out: bfloat16 [2, 2048, 768], P('dp', 'ctx')
- grad_hidden: bfloat16 [2, 2048, 768], P('dp', 'ctx')
- grad_encoder: bfloat16 [2, 2048, 768], P('dp', 'ctx')
- grad_gain_self: float32 [768], replicated
- grad_gain_cross: float32 [768], replicated
- grad_gain_feed: float32 [768], replicated
- grad_self_query: float32 [768, 768], P(None, 'tensor')
- grad_self_key: float32 [768, 768], P(None, 'tensor')
- grad_self_value: float32 [768, 768], P(None, 'tensor')
- grad_self_output: float32 [768, 768], P('tensor')
- grad_bias_table: float32 [32, 12], P(None, 'tensor')
- grad_cross_query: float32 [768, 768], P(None, 'tensor')
- grad_cross_key: float32 [768, 768], P(None, 'tensor')
- grad_cross_value: float32 [768, 768], P(None, 'tensor')
- grad_cross_output: float32 [768, 768], P('tensor')
- grad_hidden_up: float32 [768, 3072], P(None, 'tensor')
- grad_hidden_down: float32 [3072, 768], P('tensor')
Inputs may be any that keep to these rules, and one draw needn't show every extreme that they name: `dec_segments`: in each row the document numbers never fall and each of 0 to 7 appears. `enc_segments`: in each row the document numbers never fall and each of 0 to 7 appears; decoder document d of a row reads encoder document d of the same row.
All inputs are finite; a program needn't handle non-finite values.
Results may differ from a plain program's by a relative error of at most 0.023.
Values may be sent and summed in bfloat16 or wider, within the bound.
No kernel may reach another device: no remote copies, remote signals or barrier semaphores. Data moves between devices by JAX's collectives and lax.ppermute only.
A program may use at most 192 MiB of HBM per device.

v0:
```python
import math

import jax
import jax.numpy as jnp
from jax import lax
from jax.sharding import PartitionSpec as P

BUCKETS = 32
MAXDIST = 128


EPSILON = 1e-06
MASKED = -1000000000.0
HIGHEST = lax.Precision.HIGHEST
CURVE_SCALE = math.sqrt(2.0 / math.pi)
CUBIC_TERM = 0.044715


def smooth_gate(values):
    return (
        0.5
        * values
        * (1.0 + jnp.tanh(CURVE_SCALE * (values + CUBIC_TERM * values * values * values)))
    )


def smooth_slope(values):
    bent = jnp.tanh(CURVE_SCALE * (values + CUBIC_TERM * values * values * values))
    return 0.5 * (1.0 + bent) + 0.5 * values * (1.0 - bent * bent) * CURVE_SCALE * (
        1.0 + 3.0 * CUBIC_TERM * values * values
    )


def position_bucket(distance):
    exact_cut = BUCKETS // 2
    if distance < exact_cut:
        return distance
    scaled = math.log(distance / exact_cut) / math.log(MAXDIST / exact_cut) * (BUCKETS - exact_cut)
    return min(exact_cut + int(scaled), BUCKETS - 1)


def bucket_bounds():
    thresholds = []
    for target in range(1, BUCKETS):
        distance = 0
        while position_bucket(distance) < target:
            distance = distance + 1
        thresholds.append(distance)
    return thresholds


def bucket_of(distance):
    buckets = jnp.zeros(distance.shape, jnp.int32)
    for threshold in bucket_bounds():
        buckets = buckets + (distance >= threshold).astype(jnp.int32)
    return buckets


def position_table(bias_rows, offset, row_count, col_count):
    span_len = row_count + col_count - 1
    places = jnp.arange(span_len, dtype=jnp.int32)
    buckets = bucket_of(jnp.maximum(offset + row_count - 1 - places, 0))
    onehot = (buckets[:, None] == jnp.arange(BUCKETS, dtype=jnp.int32)[None, :]).astype(jnp.float32)
    by_distance = jnp.dot(onehot, bias_rows, precision=HIGHEST).T
    repeated = jnp.tile(by_distance, (1, row_count + 1))
    sheared = repeated[:, row_count - 1 : row_count - 1 + row_count * (span_len - 1)]
    sheared = sheared.reshape(by_distance.shape[0], row_count, span_len - 1)
    return sheared[:, :, :col_count]


def norm_forward(values, gain):
    scale = lax.rsqrt(jnp.mean(values * values, axis=-1, keepdims=True) + EPSILON)
    plain = values * scale
    return (plain, scale, (plain * gain).astype(jnp.bfloat16))


def norm_backward(grad_normed, plain, scale, gain):
    grad_plain = grad_normed * gain
    inner = jnp.mean(grad_plain * plain, axis=-1, keepdims=True)
    return (scale * (grad_plain - plain * inner), jnp.sum(grad_normed * plain, axis=0))


def project(left, right):
    return jnp.dot(left, right, preferred_element_type=jnp.float32)


def project_back(left, right):
    return lax.dot_general(
        left, right, (((1,), (1,)), ((), ())), preferred_element_type=jnp.float32
    )


def weight_grad(left, right):
    return lax.dot_general(
        left, right, (((0,), (0,)), ((), ())), preferred_element_type=jnp.float32
    )


def row_slice(values, start, count):
    return lax.dynamic_slice_in_dim(values, start, count, 0)


def split_heads(flat, head_count):
    return flat.reshape(flat.shape[0], flat.shape[1], head_count, flat.shape[2] // head_count)


def score_block(queries, key_rows, head_count, position_bias, allowed):
    scores = jnp.einsum(
        "sqhd,skhd->shqk",
        split_heads(queries, head_count),
        split_heads(key_rows, head_count),
        preferred_element_type=jnp.float32,
    )
    return jnp.where(allowed[:, None], scores + position_bias, MASKED)


def attend_forward(queries, key_rows, values, head_count, position_bias, allowed):
    scores = score_block(queries, key_rows, head_count, position_bias, allowed)
    highest = jnp.max(scores, axis=-1, keepdims=True)
    log_total = highest + jnp.log(jnp.sum(jnp.exp(scores - highest), axis=-1, keepdims=True))
    weights_low = jnp.exp(scores - log_total).astype(jnp.bfloat16)
    mixed_rows = jnp.einsum(
        "shqk,skhd->sqhd",
        weights_low,
        split_heads(values, head_count),
        preferred_element_type=jnp.float32,
    )
    flat = mixed_rows.reshape(mixed_rows.shape[0] * mixed_rows.shape[1], -1).astype(jnp.bfloat16)
    return (flat, log_total)


def attend_back(
    queries, key_rows, values, head_count, position_bias, allowed, log_total, grad_mixed
):
    scores = score_block(queries, key_rows, head_count, position_bias, allowed)
    weights = jnp.exp(scores - log_total)
    grad_heads = split_heads(grad_mixed, head_count)
    grad_weights = jnp.einsum(
        "sqhd,skhd->shqk",
        grad_heads,
        split_heads(values, head_count),
        preferred_element_type=jnp.float32,
    )
    inner = jnp.sum(weights * grad_weights, axis=-1, keepdims=True)
    grad_scores = (weights * (grad_weights - inner)).astype(jnp.bfloat16)
    grad_queries = jnp.einsum(
        "shqk,skhd->sqhd",
        grad_scores,
        split_heads(key_rows, head_count),
        preferred_element_type=jnp.float32,
    )
    grad_keys = jnp.einsum(
        "shqk,sqhd->skhd",
        grad_scores,
        split_heads(queries, head_count),
        preferred_element_type=jnp.float32,
    )
    grad_values = jnp.einsum(
        "shqk,sqhd->skhd",
        weights.astype(jnp.bfloat16),
        grad_heads,
        preferred_element_type=jnp.float32,
    )
    seq_rows = queries.shape[0]
    grad_queries = grad_queries.reshape(seq_rows * queries.shape[1], -1).astype(jnp.bfloat16)
    grad_keys = grad_keys.reshape(seq_rows, key_rows.shape[1], -1)
    grad_values = grad_values.reshape(seq_rows, key_rows.shape[1], -1)
    return (grad_queries, grad_keys, grad_values, grad_scores)


def body(
    hidden_in,
    encoder_out,
    dec_segments,
    enc_segments,
    gain_self,
    gain_cross,
    gain_feed,
    self_query,
    self_key,
    self_value,
    self_output,
    bias_table,
    cross_query,
    cross_key,
    cross_value,
    cross_output,
    hidden_up,
    hidden_down,
    out_grad,
):
    seq_rows, tok_len, model_width = hidden_in.shape
    head_count = bias_table.shape[1]
    offset = lax.axis_index("ctx") * tok_len
    length = tok_len * lax.axis_size("ctx")
    row_total = seq_rows * tok_len
    first_row = 0

    def own_rows(values):
        return row_slice(values, first_row, row_total)

    def head_total(term_fn):
        return lax.psum(term_fn(0, row_total), "tensor")

    tokens = hidden_in.reshape(row_total, model_width).astype(jnp.float32)
    encoded = encoder_out.reshape(row_total, model_width)
    own_ids = lax.dynamic_slice_in_dim(dec_segments, offset, tok_len, 1)
    query_places = offset + jnp.arange(tok_len, dtype=jnp.int32)
    key_places = jnp.arange(length, dtype=jnp.int32)
    causal = query_places[:, None] >= key_places[None, :]
    self_allowed = causal[None] & (own_ids[:, :, None] == dec_segments[:, None, :])
    cross_allowed = own_ids[:, :, None] == enc_segments[:, None, :]
    bias_rows = bias_table.astype(jnp.float32)
    position_bias, table_pullback = jax.vjp(
        lambda rows_in: position_table(rows_in, offset, tok_len, length), bias_rows
    )
    gain_one = gain_self.astype(jnp.float32)
    gain_two = gain_cross.astype(jnp.float32)
    gain_three = gain_feed.astype(jnp.float32)
    plain_self, scale_self, normed_self = norm_forward(tokens, gain_one)
    queries = project(normed_self, self_query).astype(jnp.bfloat16).reshape(seq_rows, tok_len, -1)
    key_rows = project(normed_self, self_key).astype(jnp.bfloat16).reshape(seq_rows, tok_len, -1)
    values = project(normed_self, self_value).astype(jnp.bfloat16).reshape(seq_rows, tok_len, -1)
    keys_all, values_all = (
        lax.all_gather(key_rows, "ctx", axis=1, tiled=True),
        lax.all_gather(values, "ctx", axis=1, tiled=True),
    )
    mixed_self, total_self = attend_forward(
        queries, keys_all, values_all, head_count, position_bias, self_allowed
    )
    after_self = own_rows(tokens) + head_total(
        lambda start, count: project(row_slice(mixed_self, start, count), self_output)
    )
    plain_cross, scale_cross, normed_cross_own = norm_forward(after_self, gain_two)
    cross_queries = (
        project(normed_cross_own, cross_query).astype(jnp.bfloat16).reshape(seq_rows, tok_len, -1)
    )
    cross_keys = project(encoded, cross_key).astype(jnp.bfloat16).reshape(seq_rows, tok_len, -1)
    cross_values = project(encoded, cross_value).astype(jnp.bfloat16).reshape(seq_rows, tok_len, -1)
    cross_keys_all, cross_values_all = (
        lax.all_gather(cross_keys, "ctx", axis=1, tiled=True),
        lax.all_gather(cross_values, "ctx", axis=1, tiled=True),
    )
    mixed_cross, total_cross = attend_forward(
        cross_queries, cross_keys_all, cross_values_all, head_count, 0.0, cross_allowed
    )
    after_cross = after_self + head_total(
        lambda start, count: project(row_slice(mixed_cross, start, count), cross_output)
    )
    plain_feed, scale_feed, normed_feed_own = norm_forward(after_cross, gain_three)
    pre_act = project(normed_feed_own, hidden_up)
    active = smooth_gate(pre_act).astype(jnp.bfloat16)
    final = after_cross + head_total(
        lambda start, count: project(row_slice(active, start, count), hidden_down)
    )
    layer_own = final.astype(jnp.bfloat16)
    grad_rows = out_grad.reshape(row_total, model_width)
    grad_hidden_down = weight_grad(active, grad_rows)
    grad_active = project_back(grad_rows, hidden_down)
    grad_pre = (grad_active * smooth_slope(pre_act)).astype(jnp.bfloat16)
    grad_hidden_up = weight_grad(normed_feed_own, grad_pre)
    grad_normed_feed = head_total(
        lambda start, count: project_back(row_slice(grad_pre, start, count), hidden_up)
    )
    grad_feed_in, grad_gain_feed = norm_backward(
        grad_normed_feed, plain_feed, scale_feed, gain_three
    )
    grad_after_cross = own_rows(grad_rows).astype(jnp.float32) + grad_feed_in
    branch_cross = grad_after_cross.astype(jnp.bfloat16)
    grad_cross_output = weight_grad(mixed_cross, branch_cross)
    grad_mixed_cross = project_back(branch_cross, cross_output).astype(jnp.bfloat16)
    grad_mixed_cross = grad_mixed_cross.reshape(seq_rows, tok_len, -1)
    grad_cross_q, grad_cross_k_all, grad_cross_v_all, cross_score_grad = attend_back(
        cross_queries,
        cross_keys_all,
        cross_values_all,
        head_count,
        0.0,
        cross_allowed,
        total_cross,
        grad_mixed_cross,
    )
    grad_cross_k, grad_cross_v = (
        lax.psum_scatter(
            grad_cross_k_all.astype(jnp.bfloat16), "ctx", scatter_dimension=1, tiled=True
        ).astype(jnp.float32),
        lax.psum_scatter(
            grad_cross_v_all.astype(jnp.bfloat16), "ctx", scatter_dimension=1, tiled=True
        ).astype(jnp.float32),
    )
    grad_cross_k = grad_cross_k.astype(jnp.bfloat16).reshape(row_total, -1)
    grad_cross_v = grad_cross_v.astype(jnp.bfloat16).reshape(row_total, -1)
    grad_cross_query = weight_grad(normed_cross_own, grad_cross_q)
    grad_cross_key = weight_grad(encoded, grad_cross_k)
    grad_cross_value = weight_grad(encoded, grad_cross_v)

    def cross_terms(start, count):
        partial_norm = project_back(row_slice(grad_cross_q, start, count), cross_query)
        partial_encoder = project_back(
            row_slice(grad_cross_k, start, count), cross_key
        ) + project_back(row_slice(grad_cross_v, start, count), cross_value)
        return jnp.concatenate([partial_norm, partial_encoder], axis=1)

    combined = head_total(cross_terms)
    grad_normed_cross = combined[:, :model_width]
    encoder_own = combined[:, model_width:].astype(jnp.bfloat16)
    grad_cross_in, grad_gain_cross = norm_backward(
        grad_normed_cross, plain_cross, scale_cross, gain_two
    )
    grad_after_self = grad_after_cross + grad_cross_in
    branch_self = grad_after_self.astype(jnp.bfloat16)
    grad_self_output = weight_grad(mixed_self, branch_self)
    grad_mixed_self = project_back(branch_self, self_output).astype(jnp.bfloat16)
    grad_mixed_self = grad_mixed_self.reshape(seq_rows, tok_len, -1)
    grad_queries, grad_keys_all, grad_values_all, grad_scores = attend_back(
        queries,
        keys_all,
        values_all,
        head_count,
        position_bias,
        self_allowed,
        total_self,
        grad_mixed_self,
    )
    grad_keys, grad_values = (
        lax.psum_scatter(
            grad_keys_all.astype(jnp.bfloat16), "ctx", scatter_dimension=1, tiled=True
        ).astype(jnp.float32),
        lax.psum_scatter(
            grad_values_all.astype(jnp.bfloat16), "ctx", scatter_dimension=1, tiled=True
        ).astype(jnp.float32),
    )
    grad_keys = grad_keys.astype(jnp.bfloat16).reshape(row_total, -1)
    grad_values = grad_values.astype(jnp.bfloat16).reshape(row_total, -1)
    score_total = jnp.sum(grad_scores.astype(jnp.float32), axis=0)
    grad_bias_table = table_pullback(score_total)[0]
    grad_self_query = weight_grad(normed_self, grad_queries)
    grad_self_key = weight_grad(normed_self, grad_keys)
    grad_self_value = weight_grad(normed_self, grad_values)

    def self_terms(start, count):
        return (
            project_back(row_slice(grad_queries, start, count), self_query)
            + project_back(row_slice(grad_keys, start, count), self_key)
            + project_back(row_slice(grad_values, start, count), self_value)
        )

    grad_normed_self = head_total(self_terms)
    grad_self_in, grad_gain_self = norm_backward(
        grad_normed_self, own_rows(plain_self), own_rows(scale_self), gain_one
    )
    hidden_own = (grad_after_self + grad_self_in).astype(jnp.bfloat16)
    (
        grad_gain_self,
        grad_gain_cross,
        grad_gain_feed,
        grad_self_query,
        grad_self_key,
        grad_self_value,
        grad_self_output,
        grad_bias_table,
        grad_cross_query,
        grad_cross_key,
        grad_cross_value,
        grad_cross_output,
        grad_hidden_up,
        grad_hidden_down,
    ) = lax.psum(
        (
            grad_gain_self,
            grad_gain_cross,
            grad_gain_feed,
            grad_self_query,
            grad_self_key,
            grad_self_value,
            grad_self_output,
            grad_bias_table,
            grad_cross_query,
            grad_cross_key,
            grad_cross_value,
            grad_cross_output,
            grad_hidden_up,
            grad_hidden_down,
        ),
        ("dp", "ctx"),
    )
    layer_rows, hidden_rows, encoder_rows = (layer_own, hidden_own, encoder_own)
    layer_out = layer_rows.reshape(hidden_in.shape)
    grad_hidden = hidden_rows.reshape(hidden_in.shape)
    grad_encoder = encoder_rows.reshape(encoder_out.shape)
    return (
        layer_out,
        grad_hidden,
        grad_encoder,
        grad_gain_self,
        grad_gain_cross,
        grad_gain_feed,
        grad_self_query,
        grad_self_key,
        grad_self_value,
        grad_self_output,
        grad_bias_table,
        grad_cross_query,
        grad_cross_key,
        grad_cross_value,
        grad_cross_output,
        grad_hidden_up,
        grad_hidden_down,
    )


def solution(mesh):
    placed = (
        P("dp", "ctx", None),
        P("dp", "ctx", None),
        P("dp", None),
        P("dp", None),
        P(),
        P(),
        P(),
        P(None, "tensor"),
        P(None, "tensor"),
        P(None, "tensor"),
        P("tensor", None),
        P(None, "tensor"),
        P(None, "tensor"),
        P(None, "tensor"),
        P(None, "tensor"),
        P("tensor", None),
        P(None, "tensor"),
        P("tensor", None),
        P("dp", "ctx", None),
    )
    return jax.shard_map(
        body,
        mesh=mesh,
        in_specs=placed,
        out_specs=(
            P("dp", "ctx", None),
            P("dp", "ctx", None),
            P("dp", "ctx", None),
            P(),
            P(),
            P(),
            P(None, "tensor"),
            P(None, "tensor"),
            P(None, "tensor"),
            P("tensor", None),
            P(None, "tensor"),
            P(None, "tensor"),
            P(None, "tensor"),
            P(None, "tensor"),
            P("tensor", None),
            P(None, "tensor"),
            P("tensor", None),
        ),
        check_vma=False,
    )
```

profile of v0, /device:TPU:0, one launch (start us, length us, event | category | flops | bytes accessed | tf_op | source)
XLA Modules:
  0.0 1009.6 jit_solution(9157248324700165231)
XLA Ops:
  11.1 10.1 all-gather
  30.2 24.2 %reshape.654 = f32[3938301]{0:T(1024)} reshape(f32[3,513,2559]{2,1,0:T(8,128)} %tile.4) | data formatting | bytes 31506408
  54.3 23.8 %tile.10 = f32[3,1312767]{1,0:T(4,128)} reshape(f32[3938301]{0:T(1024)} %reshape.654) | data formatting | bytes 31506408 | tf_op jit(solution)/shard_map/jvp()/tile | solution.py:65
  78.1 21.6 %slice.17 = f32[3,1309696]{1,0:T(4,128)} slice(f32[3,1312767]{1,0:T(4,128)} %tile.10), slice={[0:3], [511:1310207]} | slice | bytes 31432704 | tf_op jit(solution)/shard_map/jvp()/slice | solution.py:66
  99.7 44.9 %reshape.656 = f32[3929088]{0:T(1024)} reshape(f32[3,1309696]{1,0:T(4,128)} %slice.17) | data formatting | bytes 31432704
  144.5 24.9 %reshape.622 = f32[3,512,2558]{2,1,0:T(8,128)} reshape(f32[3929088]{0:T(1024)} %reshape.656) | data formatting | bytes 31432704 | tf_op jit(solution)/shard_map/jvp()/reshape | solution.py:67
  170.9 9.2 all-gather.1
  199.6 9.2 all-gather.2
  208.8 9.3 all-gather.3
  218.1 49.7 %all-reduce.12.cloned.1.call-done = f32[512,768]{1,0:T(8,128)} async-done(((f32[512,768]{1,0:T(8,128)}), f32[512,768]{1,0:T(8,128)}) %all-reduce.12.cloned.1.call-update) | async-done | bytes 1572880 | tf_op jit(solution)/shard_map/psum | solution.py:203
  294.7 67.6 %all-reduce.14.cloned.1.call-done = f32[512,768]{1,0:T(8,128)} async-done(((f32[512,768]{1,0:T(8,128)}), f32[512,768]{1,0:T(8,128)}) %all-reduce.14.cloned.1.call-update) | async-done | bytes 1572880 | tf_op jit(solution)/shard_map/psum | solution.py:203
  371.2 68.0 %all-reduce.16.cloned.1.call-done = f32[512,768]{1,0:T(8,128)} async-done(((f32[512,768]{1,0:T(8,128)}), f32[512,768]{1,0:T(8,128)}) %all-reduce.16.cloned.1.call-update) | async-done | bytes 1572880 | tf_op jit(solution)/shard_map/psum | solution.py:203
  445.1 10.5 %multiply_reduce_fusion.1 = (f32[3,512]{1,0:T(4,128)S(1)}, f32[3,512,2048]{2,1,0:T(8,128)}) fusion(f32[3,512,2048]{2,1,0:T(8,128)} %get-tuple-element.48, f32[3,512]{1,0:T(4,128)S(1)} %log_add_fusion, pred[512,2048]{1,0:T(8,128)(4,1)S(1)} %copy-done.8, bf16[512,3,64]{0,2,1:T(8,128)(2,1)S(1)} %bitcast.218, bf16[2048,3,64]{0,2,1:T(8,128)(2,1)S(1)} %bitcast.206), kind=kOutput, calls=%fused_computation.5 | convolution fusion | flops 415234560 | bytes 27209728 | tf_op jit(solution)/shard_map/sqhd,skhd->shqk/dot_general | solution.py:138
  490.3 24.0 %reduce-scatter.7.cloned.1.call-done = bf16[1,512,192]{1,2,0:T(8,128)(2,1)} async-done(((bf16[1,2048,192]{1,2,0:T(8,128)(2,1)}), bf16[1,512,192]{1,2,0:T(8,128)(2,1)}) %reduce-scatter.7.cloned.1.call-update) | async-done | bytes 196624 | tf_op jit(solution)/shard_map/reduce_scatter | solution.py:287
  518.8 120.8 %all-reduce.18.cloned.1.call-done = f32[512,1536]{1,0:T(8,128)} async-done(((f32[512,1536]{1,0:T(8,128)}), f32[512,1536]{1,0:T(8,128)}) %all-reduce.18.cloned.1.call-update) | async-done | bytes 3145744 | tf_op jit(solution)/shard_map/psum | solution.py:203
  647.4 10.8 %multiply_reduce_fusion = (f32[3,512]{1,0:T(4,128)S(1)}, f32[3,512,2048]{2,1,0:T(8,128)}) fusion(f32[3,512,2048]{2,1,0:T(8,128)} %copy-done.2, f32[3,512]{1,0:T(4,128)S(1)} %log_add_fusion.1, bf16[512,3,64]{0,2,1:T(8,128)(2,1)S(1)} %bitcast.212, bf16[2048,3,64]{0,2,1:T(8,128)(2,1)S(1)} %bitcast.200), kind=kOutput, calls=%fused_computation.3 | convolution fusion | flops 412088832 | bytes 26161152 | tf_op jit(solution)/shard_map/sqhd,skhd->shqk/dot_general | solution.py:138
  693.5 24.1 %reduce-scatter.11.cloned.1.call-done = bf16[1,512,192]{1,2,0:T(8,128)(2,1)} async-done(((bf16[1,2048,192]{1,2,0:T(8,128)(2,1)}), bf16[1,512,192]{1,2,0:T(8,128)(2,1)}) %reduce-scatter.11.cloned.1.call-update) | async-done | bytes 196624 | tf_op jit(solution)/shard_map/reduce_scatter | solution.py:329
  736.4 15.6 %reshape.658 = bf16[3929088]{0:T(1024)(128)(2,1)} reshape(bf16[3,512,2558]{2,1,0:T(8,128)(2,1)} %pad.8) | data formatting | bytes 15716352
  752.0 10.5 %reshape.639 = bf16[3,1309696]{1,0:T(4,128)(2,1)} reshape(bf16[3929088]{0:T(1024)(128)(2,1)} %reshape.658) | data formatting | bytes 15716352 | tf_op jit(solution)/shard_map/transpose(jvp())/reshape | solution.py:67
  767.6 12.5 %pad_convert_fusion = f32[3,1312767]{1,0:T(4,128)} fusion(bf16[3,1309696]{1,0:T(4,128)(2,1)} %reshape.639), kind=kLoop, calls=%fused_computation.11 | loop fusion | flops 3938301 | bytes 23611380 | tf_op jit(solution)/shard_map/transpose(jvp())/reshape | solution.py:65
  780.2 46.9 %reshape.660 = f32[3938301]{0:T(1024)} reshape(f32[3,1312767]{1,0:T(4,128)} %pad_convert_fusion) | data formatting | bytes 31506408
  827.1 25.6 %reshape.644 = f32[3,513,2559]{2,1,0:T(8,128)} reshape(f32[3938301]{0:T(1024)} %reshape.660) | data formatting | bytes 31506408 | tf_op jit(solution)/shard_map/transpose(jvp())/reshape | solution.py:65
  865.2 25.3 %all-reduce.2 = (f32[768]{0:T(1024)}, f32[768]{0:T(1024)}, f32[768]{0:T(1024)}, f32[32,3]{0,1:T(4,128)}) all-reduce(f32[768]{0:T(1024)S(1)} %get-tuple-element.21, f32[768]{0:T(1024)S(1)} %copy-done.84, f32[768]{0:T(1024)S(1)} %copy-done.83, f32[32,3]{0,1:T(4,128)S(1)} %fusion.31), channel_id=1, replica_groups=mesh['dp'=2,'ctx'=4,'tensor'=4] {'dp','ctx'}, use_global_device_ids=true, to_apply=%region_23.24 | all-reduce | flops 2400 | bytes 19200 | tf_op jit(solution)/shard_map/psum | solution.py:368
  894.5 96.3 %all-reduce.20.cloned.1.call-done = (f32[768,192]{0,1:T(8,128)}, f32[768,192]{0,1:T(8,128)}, f32[768,192]{0,1:T(8,128)}, f32[192,768]{1,0:T(8,128)}, f32[768,192...) async-done(((f32[768,192]{0,1:T(8,128)}, f32[768,192]{0,1:T(8,128)}, ...) | async-done | bytes 9437200 | tf_op jit(solution)/shard_map/psum | solution.py:368
  (313 shorter events, 208.8 us)
Async XLA Ops:
  7.2 357.9 %copy-start = (bf16[768,768]{1,0:T(8,128)(2,1)S(1)}, bf16[768,768]{1,0:T(8,128)(2,1)}, u32[]{:S(2)}) copy-start(bf16[768,768]{1,0:T(8,128)(2,1)} %param.35) | copy-start | bytes 3538948
  7.2 260.7 %all-reduce.12.cloned.1.call-start = ((), (), s32[]{:S(2)}) async-start(), calls=%async_computation.4 | async-start | bytes 3145728 | tf_op jit(solution)/shard_map/psum | solution.py:203
  8.0 161.9 %copy-start.79 = (f32[768]{0:T(1024)}, f32[768]{0:T(1024)S(1)}, u32[]{:S(2)}) copy-start(f32[768]{0:T(1024)S(1)} %convert_element_type.462) | copy-start | bytes 9220
  9.4 160.5 %copy-start.81 = (f32[512]{0:T(512)}, f32[512]{0:T(512)S(1)}, u32[]{:S(2)}) copy-start(f32[512]{0:T(512)S(1)} %add_rsqrt_fusion.2) | copy-start | bytes 6148
  21.2 169.2 %copy-start.16 = (bf16[2048,192]{0,1:T(8,128)(2,1)}, bf16[2048,192]{0,1:T(8,128)(2,1)S(1)}, u32[]{:S(2)}) copy-start(bf16[2048,192]{0,1:T(8,128)(2,1)S(1)} %all-gather) | copy-start | bytes 2359300
  181.9 104.2 %copy-start.7 = (pred[512,2048]{1,0:T(8,128)(4,1)}, pred[512,2048]{1,0:T(8,128)(4,1)S(1)}, u32[]{:S(2)}) copy-start(pred[512,2048]{1,0:T(8,128)(4,1)S(1)} %get-tuple-element.43) | copy-start | bytes 3145732
  197.7 164.7 %all-reduce.14.cloned.1.call-start = ((), (), s32[]{:S(2)}) async-start(), calls=%async_computation.5 | async-start | bytes 3145728 | tf_op jit(solution)/shard_map/psum | solution.py:203
  197.8 72.0 %copy-start.69 = (f32[768]{0:T(1024)}, f32[768]{0:T(1024)S(1)}, u32[]{:S(2)}) copy-start(f32[768]{0:T(1024)S(1)} %convert_element_type.504) | copy-start | bytes 9220
  218.1 52.8 %copy-start.35 = (bf16[768,192]{0,1:T(8,128)(2,1)S(1)}, bf16[768,192]{0,1:T(8,128)(2,1)}, u32[]{:S(2)}) copy-start(bf16[768,192]{0,1:T(8,128)(2,1)} %param.31) | copy-start | bytes 884740
  294.1 145.2 %all-reduce.16.cloned.1.call-start = ((), (), s32[]{:S(2)}) async-start(), calls=%async_computation.6 | async-start | bytes 3145728 | tf_op jit(solution)/shard_map/psum | solution.py:203
  370.9 68.3 %copy-start.72 = (f32[768]{0:T(1024)S(1)}, f32[768]{0:T(1024)}, u32[]{:S(2)}) copy-start(f32[768]{0:T(1024)} %convert_element_type.513) | copy-start | bytes 9220
  370.9 68.3 %copy-start.75 = (f32[512]{0:T(512)S(1)}, f32[512]{0:T(512)}, u32[]{:S(2)}) copy-start(f32[512]{0:T(512)} %copy-done.74) | copy-start | bytes 6148
  370.9 70.9 %copy-start.49 = (bf16[1,512,768]{2,1,0:T(8,128)(2,1)S(1)}, bf16[1,512,768]{2,1,0:T(8,128)(2,1)}, u32[]{:S(2)}) copy-start(bf16[1,512,768]{2,1,0:T(8,128)(2,1)} %param.37) | copy-start | bytes 2359300
  370.9 116.9 %reduce-scatter.5.cloned.1.call-start = ((), (), s32[]{:S(2)}) async-start(), calls=%async_computation.7 | async-start | bytes 983040 | tf_op jit(solution)/shard_map/reduce_scatter | solution.py:284
  465.3 48.9 %reduce-scatter.7.cloned.1.call-start = ((), (), s32[]{:S(2)}) async-start(), calls=%async_computation.8 | async-start | bytes 983040 | tf_op jit(solution)/shard_map/reduce_scatter | solution.py:287
  474.1 165.4 %all-reduce.18.cloned.1.call-start = ((), (), s32[]{:S(2)}) async-start(), calls=%async_computation.9 | async-start | bytes 6291456 | tf_op jit(solution)/shard_map/psum | solution.py:203
  479.3 34.9 %copy-start.34 = (bf16[768,192]{0,1:T(8,128)(2,1)S(1)}, bf16[768,192]{0,1:T(8,128)(2,1)}, u32[]{:S(2)}) copy-start(bf16[768,192]{0,1:T(8,128)(2,1)} %param.33) | copy-start | bytes 884740
  518.3 121.3 %copy-start.70 = (f32[768]{0:T(1024)S(1)}, f32[768]{0:T(1024)}, u32[]{:S(2)}) copy-start(f32[768]{0:T(1024)} %copy-done.69) | copy-start | bytes 9220
  518.3 121.3 %copy-start.78 = (f32[512]{0:T(512)S(1)}, f32[512]{0:T(512)}, u32[]{:S(2)}) copy-start(f32[512]{0:T(512)} %copy-done.77) | copy-start | bytes 6148
  518.3 172.7 %reduce-scatter.9.cloned.1.call-start = ((), (), s32[]{:S(2)}) async-start(), calls=%async_computation.10 | async-start | bytes 983040 | tf_op jit(solution)/shard_map/reduce_scatter | solution.py:326
  668.7 49.0 %reduce-scatter.11.cloned.1.call-start = ((), (), s32[]{:S(2)}) async-start(), calls=%async_computation.11 | async-start | bytes 983040 | tf_op jit(solution)/shard_map/reduce_scatter | solution.py:329
  676.3 186.9 %all-reduce.22.cloned.1.call-start = ((), (), s32[]{:S(2)}) async-start(), calls=%async_computation.13 | async-start | bytes 6291456 | tf_op jit(solution)/shard_map/psum | solution.py:203
  685.3 32.3 %copy-start.62 = (bf16[768,192]{0,1:T(8,128)(2,1)S(1)}, bf16[768,192]{0,1:T(8,128)(2,1)}, u32[]{:S(2)}) copy-start(bf16[768,192]{0,1:T(8,128)(2,1)} %param.28) | copy-start | bytes 884740
  721.2 269.7 %all-reduce.20.cloned.1.call-start = ((), (), s32[]{:S(2)}) async-start(), calls=%async_computation.12 | async-start | bytes 18874368 | tf_op jit(solution)/shard_map/psum | solution.py:368
  (87 other events, 457.4 us)
Sparse Core Ops, SparseCore 0:
  197.8 69.9 all-reduce.11
  294.2 68.1 all-reduce.13
  371.0 68.1 all-reduce.15
  465.4 22.3 reduce-scatter.4
  490.9 23.2 reduce-scatter.6
  518.4 121.1 all-reduce.17
  668.8 22.2 reduce-scatter.8
  694.3 23.2 reduce-scatter.10
  721.2 121.4 all-reduce.21
  849.7 141.0 all-reduce.19
where the time goes:
time: 1020 us; the launch traced here: 1010 us
  waiting for transfers between devices  462 us (45%)
  local copies, waits for them, and re-layouts  277 us (27%)
  matrix products  124 us (12%)
  other arithmetic  67.7 us (7%)
  blocking collectives  63.1 us (6%)
  between operations  15.3 us (2%)
    psum x5, waiting for transfers between devices, head_total(): return lax.psum(term_fn(0, row_total), 'tensor')  306 us
    unnamed x216, local copies, waits for them, and re-layouts  157 us
    psum x1, waiting for transfers between devices, body(): lax.psum((grad_gain_self, grad_gain_cross, grad_gain_feed, grad_self_quer...  96.3 us
    reshape x2, local copies, waits for them, and re-layouts, position_table(): sheared = sheared.reshape(by_distance.shape[0], row_count, span_len - 1)  35.4 us
    another operation x2, local copies, waits for them, and re-layouts, position_table(): repeated = jnp.tile(by_distance, (1, row_count + 1))  31.3 us
    reshape x1, local copies, waits for them, and re-layouts, position_table(): repeated = jnp.tile(by_distance, (1, row_count + 1))  25.6 us
    psum x1, blocking collectives, body(): lax.psum((grad_gain_self, grad_gain_cross, grad_gain_feed, grad_self_quer...  25.3 us
    reduce_scatter x1, waiting for transfers between devices, body(): lax.psum_scatter(grad_values_all.astype(jnp.bfloat16), 'ctx', scatter_dim...  24.1 us
  transfers between devices with their start and end apart: 10, of which 9 were waited for; matrix products, arithmetic and copies ran while one was open for 19% of the time, Pallas kernels for 0%

commit v1 on v0

v1 whole, which is shorter than its diff:
```python
import math
import functools
import numpy as np
import jax
import jax.numpy as jnp
from jax import lax
from jax.sharding import PartitionSpec as P
from jax.experimental import pallas as pl
from jax.experimental.pallas import tpu as pltpu

BUCKETS = 32
MAXDIST = 128
DOCS = 8
EPSILON = 1e-06
MASKED = -1000000000.0
MASK_WEIGHT = -float(2**30)
CURVE_SCALE = math.sqrt(2.0 / math.pi)
CUBIC_TERM = 0.044715
HIGHEST = lax.Precision.HIGHEST

HEAD = 64
KEYS = 256
WIDE = 256
SPAN = 1280
VMEM_BYTES = 60 * 1024 * 1024


def position_bucket(distance):
    exact_cut = BUCKETS // 2
    if distance < exact_cut:
        return distance
    scaled = math.log(distance / exact_cut) / math.log(MAXDIST / exact_cut) * (BUCKETS - exact_cut)
    return min(exact_cut + int(scaled), BUCKETS - 1)


def span_onehot():
    table = np.zeros((SPAN, BUCKETS), np.float32)
    for place in range(KEYS, KEYS + 3 * KEYS):
        table[place, position_bucket(place - KEYS)] = 1.0
    return table


def dot_nt(left, right):
    return lax.dot_general(left, right, (((1,), (1,)), ((), ())), preferred_element_type=jnp.float32)


def dot_nn(left, right):
    return lax.dot_general(left, right, (((1,), (0,)), ((), ())), preferred_element_type=jnp.float32)


def onehot_rows(count, first, meta, base):
    lane = lax.broadcasted_iota(jnp.int32, (1, HEAD), 1)
    low = jnp.zeros((1, HEAD), jnp.int32)
    high = jnp.zeros((1, HEAD), jnp.int32)
    for d in range(DOCS):
        low = jnp.where(lane == d, meta[base + d], low)
        high = jnp.where(lane == d, meta[base + d + 1], high)
    place = lax.broadcasted_iota(jnp.int32, (count, HEAD), 0) + first
    return (place >= low) & (place < high)


def head_mask(width, first, head, feature_from):
    lane = lax.broadcasted_iota(jnp.int32, (1, width), 1)
    start = first + head * HEAD
    keep = (lane >= start) & (lane < start + HEAD)
    if feature_from is not None:
        keep = keep | (lane >= feature_from)
    return keep.astype(jnp.float32).astype(jnp.bfloat16)


def gather_blocks(meta, parts, kvs, kext, key_base):
    rows = parts[0].shape[0]
    me = meta[1]
    inner = kext.shape[1] - HEAD
    for r, part in enumerate(parts):
        at = pl.multiple_of(jnp.bitwise_xor(me, r) * rows, rows)
        kvs[pl.ds(at, rows), :] = part[...]
        kext[pl.ds(at, rows), 0:inner] = part[:, 0:inner]
        kext[pl.ds(at, rows), inner:] = onehot_rows(rows, at, meta, key_base).astype(jnp.float32).astype(jnp.bfloat16)


def query_heads(meta, q_ref, qx, qm, heads, query_base):
    rows, inner = q_ref.shape
    own = onehot_rows(rows, meta[0], meta, query_base)
    qx[:, 0:inner] = q_ref[...]
    qx[:, inner:] = jnp.where(own, 0.0, MASK_WEIGHT).astype(jnp.bfloat16)
    for h in range(heads):
        qm[h] = qx[...] * head_mask(qx.shape[1], 0, h, inner)


def bias_tiles(u_ref, tile, heads):
    for h in range(heads):
        row = jnp.broadcast_to(u_ref[h : h + 1, :], (KEYS, SPAN))
        tile[h] = pltpu.roll(row, 0, 1, stride=1, stride_axis=0)[:, 0 : 4 * KEYS]


def key_range(meta, rows, query_base, key_base):
    first = meta[0]
    last = first + rows - 1
    low = meta[key_base]
    high = meta[key_base + 1]
    for d in range(1, DOCS):
        low = jnp.where(meta[query_base + d] <= first, meta[key_base + d], low)
        high = jnp.where(meta[query_base + d] <= last, meta[key_base + d + 1], high)
    return lax.div(low, KEYS), lax.div(high + KEYS - 1, KEYS)


def for_blocks(meta, rows, causal, query_base, key_base, step):
    low, high = key_range(meta, rows, query_base, key_base)
    if not causal:
        lax.fori_loop(low, high, lambda kb, c: (step(kb, None), c)[1], 0)
        return
    near = lax.div(meta[0], KEYS)
    lax.fori_loop(low, near - 1, lambda kb, c: (step(kb, None), c)[1], 0)

    @pl.when(near > 0)
    def _():
        step(near - 1, 2 * KEYS)

    step(near, KEYS)
    step(near + 1, 0)


def forward_kernel(causal, heads, count, meta, *refs):
    if causal:
        u_ref, q_ref = refs[0], refs[1]
        refs = refs[2:]
    else:
        q_ref = refs[0]
        refs = refs[1:]
    parts, refs = refs[:count], refs[count:]
    out_ref, lse_ref, kvs, kext, vt, qx, qm, ot, top, total = refs[:10]
    query_base = 2
    key_base = 2 if causal else 2 + DOCS + 1
    rows = q_ref.shape[0]
    gather_blocks(meta, parts, kvs, kext, key_base)
    query_heads(meta, q_ref, qx, qm, heads, query_base)
    lanes = kvs.shape[1]
    for kb in range(kvs.shape[0] // KEYS):
        vt[kb] = kvs[kb * KEYS : (kb + 1) * KEYS, lanes - WIDE :].T
    if causal:
        tile = refs[10]
        bias_tiles(u_ref, tile, heads)
    top[...] = jnp.full_like(top, -3e38)
    total[...] = jnp.zeros_like(total)
    ot[...] = jnp.zeros_like(ot)
    shift = WIDE - heads * HEAD

    def step(kb, place):
        kx = kext[pl.ds(pl.multiple_of(kb * KEYS, KEYS), KEYS), :]
        for h in range(heads):
            scores = dot_nt(kx, qm[h])
            far = 0.0
            if place is not None:
                scores = scores + tile[h, :, place : place + rows]
            elif causal:
                far = u_ref[h : h + 1, 4 * KEYS - 1 : 4 * KEYS]
            before = top[h : h + 1, :]
            after = jnp.maximum(before, jnp.max(scores, axis=0, keepdims=True) + far)
            scale = jnp.exp(before - after)
            weights = jnp.exp(scores - (after - far))
            top[h : h + 1, :] = after
            total[h : h + 1, :] = total[h : h + 1, :] * scale + jnp.sum(weights, axis=0, keepdims=True)
            own = vt[kb, shift + h * HEAD : shift + (h + 1) * HEAD, :]
            at = slice(h * HEAD, (h + 1) * HEAD)
            ot[at, :] = ot[at, :] * scale + dot_nn(own, weights.astype(jnp.bfloat16))

    for_blocks(meta, rows, causal, query_base, key_base, step)
    for h in range(heads):
        at = slice(h * HEAD, (h + 1) * HEAD)
        out_ref[at, :] = (ot[at, :] / total[h : h + 1, :]).astype(jnp.bfloat16)
    lse_ref[...] = top[...] + jnp.log(total[...])


def attend(causal, heads, meta, u, queries, parts):
    rows, inner = queries.shape
    part_rows, lanes = parts[0].shape
    count = len(parts)
    length = part_rows * count
    smem = pl.BlockSpec(memory_space=pltpu.SMEM)
    vmem = pl.BlockSpec(memory_space=pltpu.VMEM)
    given = ([u] if causal else []) + [queries] + list(parts)
    scratch = [
        pltpu.VMEM((length, lanes), jnp.bfloat16),
        pltpu.VMEM((length, inner + HEAD), jnp.bfloat16),
        pltpu.VMEM((length // KEYS, WIDE, KEYS), jnp.bfloat16),
        pltpu.VMEM((rows, inner + HEAD), jnp.bfloat16),
        pltpu.VMEM((heads, rows, inner + HEAD), jnp.bfloat16),
        pltpu.VMEM((inner, rows), jnp.float32),
        pltpu.VMEM((8, rows), jnp.float32),
        pltpu.VMEM((8, rows), jnp.float32),
    ]
    if causal:
        scratch.append(pltpu.VMEM((heads, KEYS, 4 * KEYS), jnp.float32))
    return pl.pallas_call(
        functools.partial(forward_kernel, causal, heads, count),
        out_shape=(
            jax.ShapeDtypeStruct((inner, rows), jnp.bfloat16),
            jax.ShapeDtypeStruct((8, rows), jnp.float32),
        ),
        in_specs=[smem] + [vmem] * len(given),
        out_specs=(vmem, vmem),
        scratch_shapes=scratch,
        compiler_params=pltpu.CompilerParams(vmem_limit_bytes=VMEM_BYTES),
        name="self_forward" if causal else "cross_forward",
    )(meta, *given)


def fold_diagonals(values):
    half = values.shape[0] // 2
    while half >= 1:
        values = values[:half] + pltpu.roll(values[half : 2 * half], SPAN - half, 1)
        half = half // 2
    return values


def backward_kernel(causal, heads, count, meta, *refs):
    if causal:
        u_ref = refs[0]
        refs = refs[1:]
    q_ref, do_ref, mixed_ref, lse_ref = refs[:4]
    parts, refs = refs[4 : 4 + count], refs[4 + count :]
    dq_ref = refs[0]
    d_refs, refs = refs[1 : 1 + count], refs[1 + count :]
    if causal:
        dbias_ref = refs[0]
        refs = refs[1:]
    kvs, kext, kt, qx, qm, dom, ra, rb, dqt, row, dkv = refs[:11]
    query_base = 2
    key_base = 2 if causal else 2 + DOCS + 1
    rows, inner = q_ref.shape
    lanes = kvs.shape[1]
    gather_blocks(meta, parts, kvs, kext, key_base)
    query_heads(meta, q_ref, qx, qm, heads, query_base)
    for kb in range(kvs.shape[0] // KEYS):
        kt[kb] = kvs[kb * KEYS : (kb + 1) * KEYS, 0:WIDE].T
    shift = WIDE - inner
    for h in range(heads):
        dom[h] = do_ref[:, lanes - WIDE :] * head_mask(WIDE, shift, h, None)
        ra[h * rows : (h + 1) * rows, :] = q_ext_only(qx, h, inner)
    ra[heads * rows :, :] = do_ref[:, 0:WIDE] * head_mask(WIDE, inner, 0, None)
    for h in range(1, heads):
        rb[(h - 1) * rows : h * rows, :] = do_ref[:, WIDE:] * head_mask(lanes - WIDE, inner - WIDE, h, None)
    turned = do_ref[:, lanes - WIDE :].astype(jnp.float32).T
    inner_sum = turned[shift:, :] * mixed_ref[...].astype(jnp.float32)
    for h in range(heads):
        row[h : h + 1, :] = jnp.sum(inner_sum[h * HEAD : (h + 1) * HEAD, :], axis=0, keepdims=True)
    dqt[...] = jnp.zeros_like(dqt)
    dkv[...] = jnp.zeros_like(dkv)
    if causal:
        tile, dtile, dfar = refs[11:14]
        bias_tiles(u_ref, tile, heads)
        dtile[...] = jnp.zeros_like(dtile)
        dfar[...] = jnp.zeros_like(dfar)

    def step(kb, place):
        at_keys = pl.ds(pl.multiple_of(kb * KEYS, KEYS), KEYS)
        kx = kext[at_keys, :]
        vx = kvs[at_keys, lanes - WIDE :]
        weights_low = []
        grads_low = []
        for h in range(heads):
            scores = dot_nt(kx, qm[h])
            lse = lse_ref[h : h + 1, :]
            if place is not None:
                scores = scores + tile[h, :, place : place + rows]
            elif causal:
                lse = lse - u_ref[h : h + 1, 4 * KEYS - 1 : 4 * KEYS]
            weights = jnp.exp(scores - lse)
            grad_weights = dot_nt(vx, dom[h])
            grads = weights * (grad_weights - row[h : h + 1, :])
            low = grads.astype(jnp.bfloat16)
            weights_low.append(weights.astype(jnp.bfloat16))
            grads_low.append(low)
            if causal:
                if place is not None:
                    dtile[h, :, place : place + rows] += low.astype(jnp.float32)
                else:
                    dfar[h : h + 1, :] += jnp.sum(low.astype(jnp.float32), axis=0, keepdims=True)
            at = slice(h * HEAD, (h + 1) * HEAD)
            dqt[at, :] += dot_nn(kt[kb, at, :], low)
        dkv[at_keys, 0:WIDE] = dot_nn(jnp.concatenate(grads_low + weights_low[:1], axis=1), ra[...]).astype(jnp.bfloat16)
        dkv[at_keys, WIDE:] = dot_nn(jnp.concatenate(weights_low[1:], axis=1), rb[...]).astype(jnp.bfloat16)

    for_blocks(meta, rows, causal, query_base, key_base, step)
    dq_ref[...] = dqt[...].astype(jnp.bfloat16)
    me = meta[1]
    part_rows = parts[0].shape[0]
    for r in range(count):
        at = pl.multiple_of(jnp.bitwise_xor(me, r) * part_rows, part_rows)
        d_refs[r][...] = dkv[pl.ds(at, part_rows), :]
    if causal:
        lane = lax.broadcasted_iota(jnp.int32, (1, SPAN), 1)
        dbias_ref[...] = jnp.zeros_like(dbias_ref)
        for h in range(heads):
            padded = jnp.concatenate([dtile[h], jnp.zeros((KEYS, SPAN - 4 * KEYS), jnp.float32)], axis=1)
            far = jnp.sum(dfar[h : h + 1, :], axis=1, keepdims=True)
            dbias_ref[h : h + 1, :] = fold_diagonals(padded) + jnp.where(lane == 4 * KEYS - 1, far, 0.0)


def q_ext_only(qx, head, inner):
    return qx[...] * head_mask(qx.shape[1], 0, head, None)


def attend_back(causal, heads, meta, u, queries, do_pad, mixed, lse, parts):
    rows, inner = queries.shape
    part_rows, lanes = parts[0].shape
    count = len(parts)
    length = part_rows * count
    smem = pl.BlockSpec(memory_space=pltpu.SMEM)
    vmem = pl.BlockSpec(memory_space=pltpu.VMEM)
    given = ([u] if causal else []) + [queries, do_pad, mixed, lse] + list(parts)
    out_shape = [jax.ShapeDtypeStruct((inner, rows), jnp.bfloat16)]
    out_shape += [jax.ShapeDtypeStruct((part_rows, lanes), jnp.bfloat16)] * count
    if causal:
        out_shape.append(jax.ShapeDtypeStruct((8, SPAN), jnp.float32))
    scratch = [
        pltpu.VMEM((length, lanes), jnp.bfloat16),
        pltpu.VMEM((length, inner + HEAD), jnp.bfloat16),
        pltpu.VMEM((length // KEYS, WIDE, KEYS), jnp.bfloat16),
        pltpu.VMEM((rows, inner + HEAD), jnp.bfloat16),
        pltpu.VMEM((heads, rows, inner + HEAD), jnp.bfloat16),
        pltpu.VMEM((heads, rows, WIDE), jnp.bfloat16),
        pltpu.VMEM(((heads + 1) * rows, WIDE), jnp.bfloat16),
        pltpu.VMEM(((heads - 1) * rows, lanes - WIDE), jnp.bfloat16),
        pltpu.VMEM((inner, rows), jnp.float32),
        pltpu.VMEM((8, rows), jnp.float32),
        pltpu.VMEM((length, lanes), jnp.bfloat16),
    ]
    if causal:
        scratch += [
            pltpu.VMEM((heads, KEYS, 4 * KEYS), jnp.float32),
            pltpu.VMEM((heads, KEYS, 4 * KEYS), jnp.float32),
            pltpu.VMEM((8, rows), jnp.float32),
        ]
    return pl.pallas_call(
        functools.partial(backward_kernel, causal, heads, count),
        out_shape=tuple(out_shape),
        in_specs=[smem] + [vmem] * len(given),
        out_specs=tuple([vmem] * len(out_shape)),
        scratch_shapes=scratch,
        compiler_params=pltpu.CompilerParams(vmem_limit_bytes=VMEM_BYTES),
        name="self_backward" if causal else "cross_backward",
    )(meta, *given)


def position_rows(bias_table, heads):
    table = span_onehot()
    rows = jnp.dot(bias_table.astype(jnp.bfloat16).T, jnp.asarray(table.T, jnp.bfloat16), preferred_element_type=jnp.float32)
    rows = rows + jnp.asarray(np.where(table.sum(1) > 0, 0.0, MASKED)[None, :], jnp.float32)
    return jnp.concatenate([rows, jnp.zeros((8 - heads, SPAN), jnp.float32)], axis=0)


def make_meta(dec_row, enc_row, offset, place):
    docs = jnp.arange(DOCS + 1, dtype=jnp.int32)
    dec = jnp.sum((dec_row[None, :] < docs[:, None]).astype(jnp.int32), axis=1)
    enc = jnp.sum((enc_row[None, :] < docs[:, None]).astype(jnp.int32), axis=1)
    return jnp.concatenate([jnp.stack([offset, place]).astype(jnp.int32), dec, enc])


def smooth_gate(values):
    return (
        0.5
        * values
        * (1.0 + jnp.tanh(CURVE_SCALE * (values + CUBIC_TERM * values * values * values)))
    )


def smooth_slope(values):
    bent = jnp.tanh(CURVE_SCALE * (values + CUBIC_TERM * values * values * values))
    return 0.5 * (1.0 + bent) + 0.5 * values * (1.0 - bent * bent) * CURVE_SCALE * (
        1.0 + 3.0 * CUBIC_TERM * values * values
    )


def norm_forward(values, gain):
    scale = lax.rsqrt(jnp.mean(values * values, axis=-1, keepdims=True) + EPSILON)
    plain = values * scale
    return (plain, scale, (plain * gain).astype(jnp.bfloat16))


def norm_backward(grad_normed, plain, scale, gain):
    grad_plain = grad_normed * gain
    inner = jnp.mean(grad_plain * plain, axis=-1, keepdims=True)
    return scale * (grad_plain - plain * inner)


def product(left, right, left_dim, right_dim):
    return lax.dot_general(
        left, right, (((left_dim,), (right_dim,)), ((), ())), preferred_element_type=jnp.float32
    )


def swap(values, axis, flip):
    count = lax.axis_size(axis)
    return lax.ppermute(values, axis, [(i, i ^ flip) for i in range(count)])


def gather_xor(values, axis):
    count = lax.axis_size(axis)
    held = {0: values}
    bit = count // 2
    while bit >= 1:
        for r in list(held):
            held[r ^ bit] = swap(held[r], axis, bit)
        bit //= 2
    return [held[r] for r in range(count)]


def scatter_xor(blocks, axis):
    count = lax.axis_size(axis)
    held = dict(enumerate(blocks))
    bit = 1
    while bit < count:
        kept = {}
        for r in held:
            if not r & bit:
                kept[r] = held[r].astype(jnp.float32) + swap(
                    held[r ^ bit].astype(jnp.bfloat16), axis, bit
                ).astype(jnp.float32)
        held = kept
        bit *= 2
    return held[0]


def scatter_rows(values, axis):
    count = lax.axis_size(axis)
    me = lax.axis_index(axis)
    rows = values.shape[0] // count
    total = lax.dynamic_slice_in_dim(values, me * rows, rows, 0)
    for flip in range(1, count):
        block = lax.dynamic_slice_in_dim(values, (me ^ flip) * rows, rows, 0)
        total = total + swap(block.astype(jnp.bfloat16), axis, flip).astype(jnp.float32)
    return total


def gather_rows(values, axis):
    return lax.all_gather(values, axis, axis=0, tiled=True)


def body(
    hidden_in,
    encoder_out,
    dec_segments,
    enc_segments,
    gain_self,
    gain_cross,
    gain_feed,
    self_query,
    self_key,
    self_value,
    self_output,
    bias_table,
    cross_query,
    cross_key,
    cross_value,
    cross_output,
    hidden_up,
    hidden_down,
    out_grad,
):
    tok_len, width = hidden_in.shape[1:]
    heads = bias_table.shape[1]
    inner = self_query.shape[1]
    low = jnp.bfloat16
    place = lax.axis_index("ctx")
    slot = lax.axis_index("tensor")
    slots = lax.axis_size("tensor")
    share = tok_len // slots
    meta = make_meta(dec_segments[0], enc_segments[0], place * tok_len, place)
    bias_rows = position_rows(bias_table, heads)
    tokens = hidden_in[0].astype(jnp.float32)
    encoded = encoder_out[0]
    cotangent = out_grad[0]
    gain_one = gain_self.astype(jnp.float32)
    gain_two = gain_cross.astype(jnp.float32)
    gain_three = gain_feed.astype(jnp.float32)

    self_output_all = gather_rows(self_output, "tensor")
    cross_query_all = gather_rows(cross_query.T, "tensor")
    cross_output_all = gather_rows(cross_output, "tensor")
    self_sides = jnp.concatenate([self_key, self_value], axis=1)
    cross_sides = jnp.concatenate([cross_key, cross_value], axis=1)
    pad = jnp.zeros((inner, width), low)

    plain_self, scale_self, normed_self = norm_forward(tokens, gain_one)
    sides = gather_xor(product(normed_self, self_sides, 1, 0).astype(low), "ctx")
    queries = product(normed_self, self_query, 1, 0).astype(low)
    cross_parts = gather_xor(product(encoded, cross_sides, 1, 0).astype(low), "ctx")
    mixed_self, lse_self = attend(True, heads, meta, bias_rows, queries, sides)
    after_self = tokens + product(gather_rows(mixed_self, "tensor"), self_output_all, 0, 0)

    plain_cross, scale_cross, normed_cross = norm_forward(after_self, gain_two)
    cross_queries = product(normed_cross, cross_query, 1, 0).astype(low)
    mixed_cross, lse_cross = attend(False, heads, meta, None, cross_queries, cross_parts)
    after_cross = after_self + product(gather_rows(mixed_cross, "tensor"), cross_output_all, 0, 0)

    plain_feed, scale_feed, normed_feed = norm_forward(after_cross, gain_three)
    pre_act = product(normed_feed, hidden_up, 1, 0)
    grad_pre = (product(cotangent, hidden_down, 1, 1) * smooth_slope(pre_act)).astype(low)
    active = smooth_gate(pre_act).astype(low)
    feed_part = product(grad_pre, hidden_up, 1, 1)
    grad_gain_feed = jnp.sum(feed_part * plain_feed, axis=0)
    feed_rows = scatter_rows(feed_part, "tensor")
    final = after_cross + lax.psum(product(active, hidden_down, 1, 0).astype(low), "tensor").astype(
        jnp.float32
    )
    layer_out = final.astype(low)
    grad_hidden_down = product(active, cotangent, 0, 0)
    grad_hidden_up = product(normed_feed, grad_pre, 0, 0)

    def own(values):
        return lax.dynamic_slice_in_dim(values, slot * share, share, 0)

    grad_rows = own(cotangent).astype(jnp.float32) + norm_backward(
        feed_rows, own(plain_feed), own(scale_feed), gain_three
    )
    branch_cross = gather_rows(grad_rows.astype(low), "tensor")
    grad_after_cross = branch_cross.astype(jnp.float32)
    grad_cross_output = product(mixed_cross, branch_cross, 1, 0)
    grad_mixed_cross = product(
        branch_cross, jnp.concatenate([pad, cross_output], axis=0), 1, 1
    ).astype(low)
    back = attend_back(
        False, heads, meta, None, cross_queries, grad_mixed_cross, mixed_cross, lse_cross, cross_parts
    )
    grad_cross_q = back[0]
    grad_cross_sides = scatter_xor(back[1:], "ctx").astype(low)
    cross_part = product(gather_rows(grad_cross_q, "tensor"), cross_query_all, 0, 0)
    grad_gain_cross = jnp.sum(cross_part * plain_cross, axis=0) * (1.0 / slots)
    grad_after_self = grad_after_cross + norm_backward(
        cross_part, plain_cross, scale_cross, gain_two
    )
    branch_self = grad_after_self.astype(low)
    grad_encoder = lax.psum(product(grad_cross_sides, cross_sides, 1, 1).astype(low), "tensor")
    grad_cross_query = product(normed_cross, grad_cross_q, 0, 1)
    grad_cross_both = product(encoded, grad_cross_sides, 0, 0)

    grad_self_output = product(mixed_self, branch_self, 1, 0)
    grad_mixed_self = product(
        branch_self, jnp.concatenate([pad, self_output], axis=0), 1, 1
    ).astype(low)
    back = attend_back(
        True, heads, meta, bias_rows, queries, grad_mixed_self, mixed_self, lse_self, sides
    )
    grad_queries = back[0]
    grad_sides = scatter_xor(back[1:-1], "ctx").astype(low)
    grad_bias = jnp.dot(
        jnp.asarray(span_onehot().T), back[-1].T, precision=HIGHEST
    )[:, :heads]
    self_part = product(grad_queries, self_query, 0, 1) + product(grad_sides, self_sides, 1, 1)
    grad_gain_self = jnp.sum(self_part * plain_self, axis=0)
    self_rows = scatter_rows(self_part, "tensor")
    hidden_rows = own(grad_after_self) + norm_backward(
        self_rows, own(plain_self), own(scale_self), gain_one
    )
    grad_hidden = gather_rows(hidden_rows.astype(low), "tensor")
    grad_self_query = product(normed_self, grad_queries, 0, 1)
    grad_self_both = product(normed_self, grad_sides, 0, 0)

    def total(values):
        return lax.psum(values.astype(low), ("dp", "ctx")).astype(jnp.float32)

    gains = lax.psum(
        jnp.stack([grad_gain_self, grad_gain_cross, grad_gain_feed]), ("dp", "ctx", "tensor")
    )
    grad_self_both = total(grad_self_both)
    grad_cross_both = total(grad_cross_both)
    return (
        layer_out[None],
        grad_hidden[None],
        grad_encoder[None],
        gains[0],
        gains[1],
        gains[2],
        total(grad_self_query),
        grad_self_both[:, :inner],
        grad_self_both[:, inner:],
        total(grad_self_output),
        lax.psum(grad_bias, ("dp", "ctx")),
        total(grad_cross_query),
        grad_cross_both[:, :inner],
        grad_cross_both[:, inner:],
        total(grad_cross_output),
        total(grad_hidden_up),
        total(grad_hidden_down),
    )


def solution(mesh):
    rows = P("dp", "ctx", None)
    ids = P("dp", None)
    columns = P(None, "tensor")
    shards = P("tensor", None)
    placed = (
        (rows, rows, ids, ids, P(), P(), P())
        + (columns, columns, columns, shards, columns, columns, columns, columns, shards)
        + (columns, shards, rows)
    )
    given = (
        (rows, rows, rows, P(), P(), P())
        + (columns, columns, columns, shards, columns, columns, columns, columns, shards)
        + (columns, shards)
    )
    return jax.shard_map(body, mesh=mesh, in_specs=placed, out_specs=given, check_vma=False)
```

time: 1020 us -> 454 us (0.45)
  waiting for transfers between devices: 462 us -> 88.8 us
  local copies, waits for them, and re-layouts: 277 us -> 18.2 us
  blocking collectives: 63.1 us -> 177 us
  matrix products: 124 us -> 41.4 us
  other arithmetic: 67.7 us -> 20.8 us
  Pallas kernels: 0 us -> 45.7 us
  starting transfers between devices: 1.2 us -> 39 us
    psum x6 -> x2, waiting for transfers between devices: 403 us -> 55.8 us  [the longest x1 55.8 us: total(): return lax.psum(values.astype(low), ('dp', 'ctx')).astype(jnp.float32)]
    unnamed x216 -> x114, local copies, waits for them, and re-layouts: 157 us -> 12.5 us
    dot_general x44 -> x26, matrix products: 124 us -> 41.4 us  [the longest x24 40.5 us: product(): lax.dot_general(left, right, (((left_dim,), (right_dim,)), ((), ())), pre...]
    all_gather x4 -> x5, blocking collectives: 37.8 us -> 110 us  [gather_rows(): return lax.all_gather(values, axis, axis=0, tiled=True)]
    reshape x4 -> x0, local copies, waits for them, and re-layouts: 63.4 us -> none  [the longest x2 35.4 us: position_table(): sheared = sheared.reshape(by_distance.shape[0], row_count, span_len - 1)]
    reduce_scatter x4 -> x0, waiting for transfers between devices: 59.2 us -> none  [the longest x1 24.1 us: body(): lax.psum_scatter(grad_values_all.astype(jnp.bfloat16), 'ctx', scatter_dim...]
    pallas_call x0 -> x4, Pallas kernels: none -> 45.7 us  [the longest x2 26.6 us: attend_back(): pl.pallas_call(functools.partial(backward_kernel, causal, heads, count),...]
    psum x1 -> x2, blocking collectives: 25.3 us -> 66.3 us  [the longest x1 53.1 us: body(): lax.psum(jnp.stack([grad_gain_self, grad_gain_cross, grad_gain_feed]), ('...]
  transfers between devices with their start and end apart: 10 -> 23, of which waited for: 9 -> 7; matrix products, arithmetic and copies ran while one was open for 19% -> 13% of each run, Pallas kernels for 0% -> 10%
where the time goes in v1:
time: 454 us; the launch traced here: 445 us
  blocking collectives  177 us (39%)
  waiting for transfers between devices  88.8 us (20%)
  Pallas kernels  45.7 us (10%)
  matrix products  41.4 us (9%)
  starting transfers between devices  39 us (9%)
  other arithmetic  20.8 us (5%)
  local copies, waits for them, and re-layouts  18.2 us (4%)
  between operations  14.7 us (3%)
    all_gather x5, blocking collectives, gather_rows(): return lax.all_gather(values, axis, axis=0, tiled=True)  110 us
    psum x1, waiting for transfers between devices, total(): return lax.psum(values.astype(low), ('dp', 'ctx')).astype(jnp.float32)  55.8 us
    psum x1, blocking collectives, body(): lax.psum(jnp.stack([grad_gain_self, grad_gain_cross, grad_gain_feed]), ('...  53.1 us
    dot_general x24, matrix products, product(): lax.dot_general(left, right, (((left_dim,), (right_dim,)), ((), ())), pre...  40.5 us
    ppermute x18, starting transfers between devices, swap(): return lax.ppermute(values, axis, [(i, i ^ flip) for i in range(count)])  38.6 us
    ppermute x18, waiting for transfers between devices, swap(): return lax.ppermute(values, axis, [(i, i ^ flip) for i in range(count)])  31.6 us
    pallas_call x2, Pallas kernels, attend_back(): pl.pallas_call(functools.partial(backward_kernel, causal, heads, count),...  26.6 us
    pallas_call x2, Pallas kernels, attend(): pl.pallas_call(functools.partial(forward_kernel, causal, heads, count), o...  19.1 us
  transfers between devices with their start and end apart: 23, of which 7 were waited for; matrix products, arithmetic and copies ran while one was open for 13% of the time, Pallas kernels for 10%

profile of v1, /device:TPU:0, one launch (start us, length us, event | category | flops | bytes accessed | tf_op | source)
XLA Modules:
  0.0 445.4 jit_solution(5143804610411658379)
XLA Ops:
  13.4 2.6 collective-permute-start.1
  19.5 6.5 %collective-permute-done.1.refs_4_.refs_7_ = bf16[512,384]{1,0:T(8,128)(2,1)S(1)} collective-permute-done((bf16[512,384]{1,0:T(8,128)(2,1)S(1)}, bf16[512,384]{1,0:T(8,128)(2,1)S(1)}, u32[]{:S(2)}, u32[]{:S(2)}) %collective-permute-start.1) | collective-permute-done | bytes 393248 | tf_op jit(solution)/shard_map/ppermute | solution.py:396
  36.1 6.0 %self_forward.1 = (bf16[192,512]{1,0:T(8,128)(2,1)}, f32[8,512]{1,0:T(8,128)}) custom-call(s32[20]{0:T(128)} %pad_add_fusion.meta, f32[8,1280]{1,0:T(8,128)} %concatenate.19.refs_0_, bf16[512,192]{1,0:T(8,128)(2,1)} %convolution_convert_fusion.15.refs_1_, bf16[512,384]{1,0:T(8,128)(2,1)} %copy-done.11, bf16[512,384]{1,0:T(8,128)(2,1)} %copy-done.12, ...), custom_call_target="tpu_custom_call" | custom-call | tf_op jit(solution)/shard_map/self_forward/pallas_call | solution.py:195
  42.0 26.4 %all_gather.24 = bf16[768,512]{1,0:T(8,128)(2,1)} all-gather(bf16[192,512]{1,0:T(8,128)(2,1)} %get-tuple-element.32.refs_3_), channel_id=1, replica_groups=mesh['dp'=2,'ctx'=4,'tensor'=4] {'tensor'}, dimensions={0}, use_global_device_ids=true | all-gather | bytes 983040 | tf_op jit(solution)/shard_map/all_gather | solution.py:438
  68.5 2.5 multiply_reduce_fusion.5
  72.1 13.2 %cross_forward.1 = (bf16[192,512]{1,0:T(8,128)(2,1)}, f32[8,512]{1,0:T(8,128)}) custom-call(s32[20]{0:T(128)} %pad_add_fusion.meta, bf16[512,192]{1,0:T(8,128)(2,1)} %convolution_convert_fusion.14.refs_0_, bf16[512,384]{1,0:T(8,128)(2,1)} %fusion.11.refs_1_.refs_4_, bf16[512,384]{1,0:T(8,128)(2,1)} %collective-permute-done.3.refs_2_.refs_5_, ...), custom_call_target="tpu_custom_call" | custom-call | tf_op jit(solution)/shard_map/cross_forward/pallas_call | solution.py:195
  85.3 28.3 %all_gather.26 = bf16[768,512]{1,0:T(8,128)(2,1)S(1)} all-gather(bf16[192,512]{1,0:T(8,128)(2,1)} %get-tuple-element.33.refs_2_), channel_id=1, replica_groups=mesh['dp'=2,'ctx'=4,'tensor'=4] {'tensor'}, dimensions={0}, use_global_device_ids=true | all-gather | bytes 983040 | tf_op jit(solution)/shard_map/all_gather | solution.py:438
  124.5 3.8 collective-permute-start.8
  133.2 10.4 %collective-permute-done.7 = bf16[128,768]{1,0:T(8,128)(2,1)S(1)} collective-permute-done((bf16[128,768]{1,0:T(8,128)(2,1)S(1)}, bf16[128,768]{1,0:T(8,128)(2,1)S(1)}, u32[]{:S(2)}, u32[]{:S(2)}) %collective-permute-start.7) | collective-permute-done | bytes 196640 | tf_op jit(solution)/shard_map/ppermute | solution.py:396
  144.1 19.5 %all_gather.28 = bf16[512,768]{1,0:T(8,128)(2,1)S(1)} all-gather(bf16[128,768]{1,0:T(8,128)(2,1)S(1)} %fusion.19), channel_id=1, replica_groups=mesh['dp'=2,'ctx'=4,'tensor'=4] {'tensor'}, dimensions={0}, use_global_device_ids=true | all-gather | bytes 983040 | tf_op jit(solution)/shard_map/all_gather | solution.py:438
  164.8 18.5 %cross_backward.1 = (bf16[192,512]{1,0:T(8,128)(2,1)}, bf16[512,384]{1,0:T(8,128)(2,1)}, bf16[512,384]{1,0:T(8,128)(2,1)}, bf16[512,384]{1,0:T(8,128)(2,1)}, bf16[512,384]{1,0:T(8,128)(2,1)}) custom-call(s32[20]{0:T(128)} %pad_add_fusion.meta, bf16[512,192]{1,0:T(8,128)(2,1)} %convolution_convert_fusion.14.refs_0_, ...), custom_call_target="tpu_custom_call" | custom-call | tf_op jit(solution)/shard_map/cross_backward/pallas_call | solution.py:336
  183.8 18.5 %all_gather.29 = bf16[768,512]{1,0:T(8,128)(2,1)S(1)} all-gather(bf16[192,512]{1,0:T(8,128)(2,1)} %get-tuple-element.35), channel_id=1, replica_groups=mesh['dp'=2,'ctx'=4,'tensor'=4] {'tensor'}, dimensions={0}, use_global_device_ids=true | all-gather | bytes 983040 | tf_op jit(solution)/shard_map/all_gather | solution.py:438
  202.3 2.9 multiply_reduce_fusion.1
  207.5 8.1 %self_backward.1 = (bf16[192,512]{1,0:T(8,128)(2,1)}, bf16[512,384]{1,0:T(8,128)(2,1)}, bf16[512,384]{1,0:T(8,128)(2,1)}, bf16[512,384]{1,0:T(8,128)(2,1)}, bf16[512,384]{1,0:T(8,128)(2,1)}, /*index=5*/f32[8,1280]{1,0:T(8,128)}) custom-call(s32[20]{0:T(128)} %pad_add_fusion.meta, f32[8,1280]{1,0:T(8,128)} %concatenate.19.refs_0_, ...), custom_call_target="tpu_custom_call" | custom-call | tf_op jit(solution)/shard_map/self_backward/pallas_call | solution.py:336
  218.6 21.7 %collective-permute-start.17 = (bf16[512,384]{1,0:T(8,128)(2,1)S(1)}, bf16[512,384]{1,0:T(8,128)(2,1)S(1)}, u32[]{:S(2)}, u32[]{:S(2)}) collective-permute-start(bf16[512,384]{1,0:T(8,128)(2,1)S(1)} %add_convert_fusion.2), channel_id=1, source_target_pairs={{0,8},{4,12},{8,0},{12,4},{1,9},{5,13},{9,1},{13,5},{2,10},{6,14},... | collective-permute-start | bytes 1179656 | tf_op jit(solution)/shard_map/ppermute | solution.py:396
  240.3 2.5 convolution_convert_fusion.11
  243.8 6.2 %collective-permute-done.17 = bf16[512,384]{1,0:T(8,128)(2,1)S(1)} collective-permute-done((bf16[512,384]{1,0:T(8,128)(2,1)S(1)}, bf16[512,384]{1,0:T(8,128)(2,1)S(1)}, u32[]{:S(2)}, u32[]{:S(2)}) %collective-permute-start.17) | collective-permute-done | bytes 393248 | tf_op jit(solution)/shard_map/ppermute | solution.py:396
  250.8 2.5 fusion.9
  261.4 6.5 %collective-permute-done.11 = bf16[512,384]{1,0:T(8,128)(2,1)S(1)} collective-permute-done((bf16[512,384]{1,0:T(8,128)(2,1)S(1)}, bf16[512,384]{1,0:T(8,128)(2,1)S(1)}, u32[]{:S(2)}, u32[]{:S(2)}) %collective-permute-start.11) | collective-permute-done | bytes 393248 | tf_op jit(solution)/shard_map/ppermute | solution.py:396
  267.9 2.5 convolution_convert_fusion.5
  271.1 13.2 %psum.90 = f32[32,3]{0,1:T(4,128)} all-reduce(f32[32,3]{0,1:T(4,128)S(1)} %fusion.23), channel_id=1, replica_groups=mesh['dp'=2,'ctx'=4,'tensor'=4] {'dp','ctx'}, use_global_device_ids=true, to_apply=%region_17.0 | all-reduce | flops 96 | bytes 768 | tf_op jit(solution)/shard_map/psum | solution.py:580
  292.2 53.1 %psum.86 = f32[3,768]{1,0:T(4,128)S(1)} all-reduce(f32[3,768]{1,0:T(4,128)S(1)} %pad_maximum_fusion), channel_id=1, replica_groups=mesh['dp'=2,'ctx'=4,'tensor'=4] {'dp','ctx','tensor'}, use_global_device_ids=true, to_apply=%region_13.0 | all-reduce | flops 2304 | bytes 18432 | tf_op jit(solution)/shard_map/psum | solution.py:564
  349.3 17.7 %all_gather.31 = bf16[512,768]{1,0:T(8,128)(2,1)S(1)} all-gather(bf16[128,768]{1,0:T(8,128)(2,1)S(1)} %add_convert_fusion.5), channel_id=1, replica_groups=mesh['dp'=2,'ctx'=4,'tensor'=4] {'tensor'}, dimensions={0}, use_global_device_ids=true | all-gather | bytes 983040 | tf_op jit(solution)/shard_map/all_gather | solution.py:438
  369.2 55.8 %all-reduce.8.cloned.1.call-done = (bf16[768,384]{1,0:T(8,128)(2,1)}, bf16[768,384]{0,1:T(8,128)(2,1)}, bf16[768,192]{0,1:T(8,128)(2,1)}, bf16[192,768]{1,0:T(8,...) async-done(((bf16[768,384]{1,0:T(8,128)(2,1)}, bf16[768,384]{0,1:T(8,128)(2,1)}, ...) | async-done | bytes 4718608 | tf_op jit(solution)/shard_map/psum | solution.py:562
  (220 shorter events, 82.0 us)
Async XLA Ops:
  7.2 109.8 %copy-start = (bf16[768,768]{1,0:T(8,128)(2,1)S(1)}, bf16[768,768]{1,0:T(8,128)(2,1)}, u32[]{:S(2)}) copy-start(bf16[768,768]{1,0:T(8,128)(2,1)} %param.38) | copy-start | bytes 3538948
  7.2 61.3 %all-gather.4.cloned.1.call-start = ((), (), s32[]{:S(2)}) async-start(), calls=%async_computation | async-start | bytes 1474560 | tf_op jit(solution)/shard_map/all_gather | solution.py:438
  8.0 105.6 %all-gather.6.cloned.1.call-start = ((), (), s32[]{:S(2)}) async-start(), calls=%async_computation.1 | async-start | bytes 1474560 | tf_op jit(solution)/shard_map/all_gather | solution.py:438
  8.7 193.6 %all-gather.8.cloned.1.call-start = ((), (), s32[]{:S(2)}) async-start(), calls=%async_computation.2 | async-start | bytes 1474560 | tf_op jit(solution)/shard_map/all_gather | solution.py:438
  12.9 21.7 %collective-permute-start = (bf16[512,384]{1,0:T(8,128)(2,1)S(1)}, bf16[512,384]{1,0:T(8,128)(2,1)S(1)}, u32[]{:S(2)}, u32[]{:S(2)}) collective-permute-start(bf16[512,384]{1,0:T(8,128)(2,1)S(1)} %convolution_convert_fusion.9.refs_2_.refs_5_), channel_id=1, source_target_pairs={{0,4},{4,0},{8,12},{12,8},{1,5},{5,1},{9,13},{13,9},{2,6},{6,2},{1... | collective-permute-start | bytes 1179656 | tf_op jit(solution)/shard_map/ppermute | solution.py:396
  13.4 12.5 %collective-permute-start.1 = (bf16[512,384]{1,0:T(8,128)(2,1)S(1)}, bf16[512,384]{1,0:T(8,128)(2,1)S(1)}, u32[]{:S(2)}, u32[]{:S(2)}) collective-permute-start(bf16[512,384]{1,0:T(8,128)(2,1)S(1)} %convolution_convert_fusion.9.refs_2_.refs_5_), channel_id=1, source_target_pairs={{0,8},{4,12},{8,0},{12,4},{1,9},{5,13},{9,1},{13,5},{2,10},{6,14},... | collective-permute-start | bytes 1179656 | tf_op jit(solution)/shard_map/ppermute | solution.py:396
  18.2 53.9 %collective-permute-start.3 = (bf16[512,384]{1,0:T(8,128)(2,1)}, bf16[512,384]{1,0:T(8,128)(2,1)}, u32[]{:S(2)}, u32[]{:S(2)}) collective-permute-start(bf16[512,384]{1,0:T(8,128)(2,1)} %fusion.11.refs_1_.refs_4_), channel_id=1, source_target_pairs={{0,4},{4,0},{8,12},{12,8},{1,5},{5,1},{9,13},{13,9},{2,6},{6,2},{1... | collective-permute-start | bytes 1179656 | tf_op jit(solution)/shard_map/ppermute | solution.py:396
  18.4 15.8 %collective-permute-start.4 = (bf16[512,384]{1,0:T(8,128)(2,1)}, bf16[512,384]{1,0:T(8,128)(2,1)}, u32[]{:S(2)}, u32[]{:S(2)}) collective-permute-start(bf16[512,384]{1,0:T(8,128)(2,1)} %fusion.11.refs_1_.refs_4_), channel_id=1, source_target_pairs={{0,8},{4,12},{8,0},{12,4},{1,9},{5,13},{9,1},{13,5},{2,10},{6,14},... | collective-permute-start | bytes 1179656 | tf_op jit(solution)/shard_map/ppermute | solution.py:396
  18.7 348.3 %all-reduce.10.cloned.1.call-start = ((), (), s32[]{:S(2)}) async-start(), calls=%async_computation.4 | async-start | bytes 3145728 | tf_op jit(solution)/shard_map/psum | solution.py:505
  26.0 8.6 %collective-permute-start.2 = (bf16[512,384]{1,0:T(8,128)(2,1)S(1)}, bf16[512,384]{1,0:T(8,128)(2,1)S(1)}, u32[]{:S(2)}, u32[]{:S(2)}) collective-permute-start(bf16[512,384]{1,0:T(8,128)(2,1)S(1)} %collective-permute-done.1.refs_4_.refs_7_), channel_id=1, source_target_pairs={{0,4},{4,0},{8,12},{12,8},{1,5},{5,1},{9,13},{13,9},{2,6},{6,2},{1... | collective-permute-start | bytes 1179656 | tf_op jit(solution)/shard_map/ppermute | solution.py:396
  34.3 37.9 %collective-permute-start.5 = (bf16[512,384]{1,0:T(8,128)(2,1)}, bf16[512,384]{1,0:T(8,128)(2,1)}, u32[]{:S(2)}, u32[]{:S(2)}) collective-permute-start(bf16[512,384]{1,0:T(8,128)(2,1)} %collective-permute-done.4.refs_3_.refs_6_), channel_id=1, source_target_pairs={{0,4},{4,0},{8,12},{12,8},{1,5},{5,1},{9,13},{13,9},{2,6},{6,2},{1... | collective-permute-start | bytes 1179656 | tf_op jit(solution)/shard_map/ppermute | solution.py:396
  124.5 8.8 %collective-permute-start.8 = (bf16[128,768]{1,0:T(8,128)(2,1)S(1)}, bf16[128,768]{1,0:T(8,128)(2,1)S(1)}, u32[]{:S(2)}, u32[]{:S(2)}) collective-permute-start(bf16[128,768]{1,0:T(8,128)(2,1)S(1)} %get-tuple-element.100), channel_id=1, source_target_pairs={{0,3},{1,2},{2,1},{3,0},{4,7},{5,6},{6,5},{7,4},{8,11},{9,10},{10,... | collective-permute-start | bytes 589832 | tf_op jit(solution)/shard_map/ppermute | solution.py:396
  128.3 15.4 %collective-permute-start.7 = (bf16[128,768]{1,0:T(8,128)(2,1)S(1)}, bf16[128,768]{1,0:T(8,128)(2,1)S(1)}, u32[]{:S(2)}, u32[]{:S(2)}) collective-permute-start(bf16[128,768]{1,0:T(8,128)(2,1)S(1)} %get-tuple-element.101), channel_id=1, source_target_pairs={{0,2},{1,3},{2,0},{3,1},{4,6},{5,7},{6,4},{7,5},{8,10},{9,11},{10,... | collective-permute-start | bytes 589832 | tf_op jit(solution)/shard_map/ppermute | solution.py:396
  128.3 15.4 %collective-permute-start.6 = (bf16[128,768]{1,0:T(8,128)(2,1)S(1)}, bf16[128,768]{1,0:T(8,128)(2,1)S(1)}, u32[]{:S(2)}, u32[]{:S(2)}) collective-permute-start(bf16[128,768]{1,0:T(8,128)(2,1)S(1)} %get-tuple-element.99), channel_id=1, source_target_pairs={{0,1},{1,0},{2,3},{3,2},{4,5},{5,4},{6,7},{7,6},{8,9},{9,8},{10,11... | collective-permute-start | bytes 589832 | tf_op jit(solution)/shard_map/ppermute | solution.py:396
  183.3 34.1 %collective-permute-start.16 = (bf16[512,384]{1,0:T(8,128)(2,1)}, bf16[512,384]{1,0:T(8,128)(2,1)}, u32[]{:S(2)}, u32[]{:S(2)}) collective-permute-start(bf16[512,384]{1,0:T(8,128)(2,1)} %get-tuple-element.45), channel_id=1, source_target_pairs={{0,4},{4,0},{8,12},{12,8},{1,5},{5,1},{9,13},{13,9},{2,6},{6,2},{1... | collective-permute-start | bytes 1179656 | tf_op jit(solution)/shard_map/ppermute | solution.py:396
  183.3 60.5 %collective-permute-start.15 = (bf16[512,384]{1,0:T(8,128)(2,1)}, bf16[512,384]{1,0:T(8,128)(2,1)}, u32[]{:S(2)}, u32[]{:S(2)}) collective-permute-start(bf16[512,384]{1,0:T(8,128)(2,1)} %get-tuple-element.43), channel_id=1, source_target_pairs={{0,4},{4,0},{8,12},{12,8},{1,5},{5,1},{9,13},{13,9},{2,6},{6,2},{1... | collective-permute-start | bytes 1179656 | tf_op jit(solution)/shard_map/ppermute | solution.py:396
  215.6 40.2 %collective-permute-start.10 = (bf16[512,384]{1,0:T(8,128)(2,1)}, bf16[512,384]{1,0:T(8,128)(2,1)}, u32[]{:S(2)}, u32[]{:S(2)}) collective-permute-start(bf16[512,384]{1,0:T(8,128)(2,1)} %get-tuple-element.41), channel_id=1, source_target_pairs={{0,4},{4,0},{8,12},{12,8},{1,5},{5,1},{9,13},{13,9},{2,6},{6,2},{1... | collective-permute-start | bytes 1179656 | tf_op jit(solution)/shard_map/ppermute | solution.py:396
  217.3 44.1 %collective-permute-start.9 = (bf16[512,384]{1,0:T(8,128)(2,1)}, bf16[512,384]{1,0:T(8,128)(2,1)}, u32[]{:S(2)}, u32[]{:S(2)}) collective-permute-start(bf16[512,384]{1,0:T(8,128)(2,1)} %get-tuple-element.39), channel_id=1, source_target_pairs={{0,4},{4,0},{8,12},{12,8},{1,5},{5,1},{9,13},{13,9},{2,6},{6,2},{1... | collective-permute-start | bytes 1179656 | tf_op jit(solution)/shard_map/ppermute | solution.py:396
  218.6 31.4 %collective-permute-start.17 = (bf16[512,384]{1,0:T(8,128)(2,1)S(1)}, bf16[512,384]{1,0:T(8,128)(2,1)S(1)}, u32[]{:S(2)}, u32[]{:S(2)}) collective-permute-start(bf16[512,384]{1,0:T(8,128)(2,1)S(1)} %add_convert_fusion.2), channel_id=1, source_target_pairs={{0,8},{4,12},{8,0},{12,4},{1,9},{5,13},{9,1},{13,5},{2,10},{6,14},... | collective-permute-start | bytes 1179656 | tf_op jit(solution)/shard_map/ppermute | solution.py:396
  253.3 171.7 %all-reduce.8.cloned.1.call-start = ((), (), s32[]{:S(2)}) async-start(), calls=%async_computation.3 | async-start | bytes 9437184 | tf_op jit(solution)/shard_map/psum | solution.py:562
  256.9 10.9 %collective-permute-start.11 = (bf16[512,384]{1,0:T(8,128)(2,1)S(1)}, bf16[512,384]{1,0:T(8,128)(2,1)S(1)}, u32[]{:S(2)}, u32[]{:S(2)}) collective-permute-start(bf16[512,384]{1,0:T(8,128)(2,1)S(1)} %add_convert_fusion.4), channel_id=1, source_target_pairs={{0,8},{4,12},{8,0},{12,4},{1,9},{5,13},{9,1},{13,5},{2,10},{6,14},... | collective-permute-start | bytes 1179656 | tf_op jit(solution)/shard_map/ppermute | solution.py:396
  287.7 58.2 %collective-permute-start.14 = (bf16[128,768]{1,0:T(8,128)(2,1)S(1)}, bf16[128,768]{1,0:T(8,128)(2,1)S(1)}, u32[]{:S(2)}, u32[]{:S(2)}) collective-permute-start(bf16[128,768]{1,0:T(8,128)(2,1)S(1)} %get-tuple-element.97), channel_id=1, source_target_pairs={{0,3},{1,2},{2,1},{3,0},{4,7},{5,6},{6,5},{7,4},{8,11},{9,10},{10,... | collective-permute-start | bytes 589832 | tf_op jit(solution)/shard_map/ppermute | solution.py:396
  290.0 55.9 %collective-permute-start.13 = (bf16[128,768]{1,0:T(8,128)(2,1)S(1)}, bf16[128,768]{1,0:T(8,128)(2,1)S(1)}, u32[]{:S(2)}, u32[]{:S(2)}) collective-permute-start(bf16[128,768]{1,0:T(8,128)(2,1)S(1)} %get-tuple-element.98), channel_id=1, source_target_pairs={{0,2},{1,3},{2,0},{3,1},{4,6},{5,7},{6,4},{7,5},{8,10},{9,11},{10,... | collective-permute-start | bytes 589832 | tf_op jit(solution)/shard_map/ppermute | solution.py:396
  290.0 55.9 %collective-permute-start.12 = (bf16[128,768]{1,0:T(8,128)(2,1)S(1)}, bf16[128,768]{1,0:T(8,128)(2,1)S(1)}, u32[]{:S(2)}, u32[]{:S(2)}) collective-permute-start(bf16[128,768]{1,0:T(8,128)(2,1)S(1)} %get-tuple-element.96), channel_id=1, source_target_pairs={{0,1},{1,0},{2,3},{3,2},{4,5},{5,4},{6,7},{7,6},{8,9},{9,8},{10,11... | collective-permute-start | bytes 589832 | tf_op jit(solution)/shard_map/ppermute | solution.py:396
  (53 other events, 332.8 us)
Sparse Core Ops, SparseCore 0:
  9.6 33.1 all-gather.3
  44.4 36.8 all-gather.5
  82.8 41.2 all-gather.7
  253.4 79.6 all-reduce.9
  338.1 86.7 all-reduce.7
